TPU v7x, 32 devices: a whole 2x2x4 slice. The times are simulated.
32 devices in a mesh: dp: 8 (over z, y), seq: 4 (over x, core).
Axes of the slice: x: 2, y: 2, z: 4, core: 2. Of those that a mesh axis runs over, the one named last changes fastest.
Arguments:
- tokens: bfloat16 [16384, 1024], P(('dp', 'seq')), may hold values from -6 to 6
- doc_starts: int32 [8, 4], P('dp'), may hold values from 0 to 2047, as said below
- routes: int32 [16384, 1], P(('dp', 'seq')), may hold values from 0 to 63; in each aligned block of 512 rows (0 to 511, 512 to 1023, ...) at most 16 rows name the same one
- ln1_gain: bfloat16 [1024], P('seq'), may hold values from 0.5 to 1.5
- ln1_bias: bfloat16 [1024], P('seq'), may hold values from -4 to 4
- w_qkv: bfloat16 [1024, 3072], P('seq'), may hold values from -0.1875 to 0.1875
- w_proj: bfloat16 [1024, 1024], P('seq'), may hold values from -0.75 to 0.75
- ln2_gain: bfloat16 [1024], P('seq'), may hold values from 0.5 to 1.5
- ln2_bias: bfloat16 [1024], P('seq'), may hold values from -4 to 4
- w_router: bfloat16 [1024, 64], P('seq'), may hold values from -0.09375 to 0.09375
- w_expert_in: bfloat16 [64, 1024, 4096], P('dp', None, 'seq'), may hold values from -0.1875 to 0.1875
- w_expert_out: bfloat16 [64, 4096, 1024], P('dp', 'seq'), may hold values from -12 to 12
- out_grad: bfloat16 [16384, 1024], P(('dp', 'seq')), may hold values from -6 to 6
Outputs:
- output: bfloat16 [16384, 1024], P(('dp', 'seq'))
- input_grad: float32 [16384, 1024], P(('dp', 'seq'))
- ln1_gain_grad: float32 [1024], P('seq')
- ln1_bias_grad: float32 [1024], P('seq')
- w_qkv_grad: float32 [1024, 3072], P('seq')
- w_proj_grad: float32 [1024, 1024], P('seq')
- ln2_gain_grad: float32 [1024], P('seq')
- ln2_bias_grad: float32 [1024], P('seq')
- w_router_grad: float32 [1024, 64], P('seq')
- w_expert_in_grad: float32 [64, 1024, 4096], P('dp', None, 'seq')
- w_expert_out_grad: float32 [64, 4096, 1024], P('dp', 'seq')
Inputs may be any that keep to these rules, and one draw needn't show every extreme that they name: `doc_starts`: each row begins with 0 and rises strictly; entry j is where document j of sequence r begins. `routes`: among the 512 rows of one device (aligned blocks), no expert is named more than 16 times, a bound that some block reaches.
All inputs are finite; a program needn't handle non-finite values.
Results may differ from a plain program's by a relative error of at most 0.02.
Values may be sent and summed in bfloat16 or wider, within the bound.
A program may use at most 320 MiB of HBM per device.

v0:
```python
import jax
import jax.numpy as jnp
from jax import lax
from jax.sharding import PartitionSpec as P

H = 16
HD = 64
EXPERTS = 64
TOK_DEV = 512
EPS = 1e-05
NEG = -1e30


def normalize(values):
    center = values - jnp.mean(values, axis=-1, keepdims=True)
    inverse = lax.rsqrt(jnp.mean(center * center, axis=-1, keepdims=True) + EPS)
    return (center * inverse, inverse)


def norm_back(grad_norm, normed, inverse):
    first_mean = jnp.mean(grad_norm, axis=-1, keepdims=True)
    second_mean = jnp.mean(grad_norm * normed, axis=-1, keepdims=True)
    return inverse * (grad_norm - first_mean - normed * second_mean)


def collect_rows(rows_part, grads_part):
    return (
        lax.all_gather(rows_part, "seq", axis=1, tiled=True),
        lax.all_gather(grads_part, "seq", axis=1, tiled=True),
    )


def route_rows(rows_part, grads_part):
    return (
        lax.all_to_all(rows_part, "dp", split_axis=0, concat_axis=0, tiled=True),
        lax.all_to_all(grads_part, "dp", split_axis=0, concat_axis=0, tiled=True),
    )


def expert_work(rows_in, grads_in, first_weight, second_weight):
    pre_act = jnp.einsum(
        "abecd,edf->abecf", rows_in, first_weight, preferred_element_type=jnp.float32
    )
    hidden_exp, gelu_back = jax.vjp(jax.nn.gelu, pre_act)
    hidden_low = hidden_exp.astype(jnp.bfloat16)
    part_out = jnp.einsum(
        "abecf,efd->abecd", hidden_low, second_weight, preferred_element_type=jnp.float32
    )
    grad_hidden = jnp.einsum(
        "abecd,efd->abecf", grads_in, second_weight, preferred_element_type=jnp.float32
    )
    grad_pre = gelu_back(grad_hidden)[0].astype(jnp.bfloat16)
    first_grad = jnp.einsum(
        "abecd,abecf->edf", rows_in, grad_pre, preferred_element_type=jnp.float32
    )
    second_grad = jnp.einsum(
        "abecf,abecd->efd", hidden_low, grads_in, preferred_element_type=jnp.float32
    )
    part_dx = jnp.einsum(
        "abecf,edf->abecd", grad_pre, first_weight, preferred_element_type=jnp.float32
    )
    return (part_out, part_dx, first_grad, second_grad)


def per_device(
    tokens,
    doc_starts,
    routes,
    ln1_gain,
    ln1_bias,
    w_qkv,
    w_proj,
    ln2_gain,
    ln2_bias,
    w_router,
    w_expert_in,
    w_expert_out,
    out_grad,
):
    seq_count = lax.axis_size("seq")
    dp_count = lax.axis_size("dp")
    gathered_weights = (
        lax.all_gather(w_qkv, "seq", axis=0, tiled=True),
        lax.all_gather(w_proj, "seq", axis=0, tiled=True),
        lax.all_gather(w_router, "seq", axis=0, tiled=True),
        lax.all_gather(ln1_gain, "seq", axis=0, tiled=True),
        lax.all_gather(ln1_bias, "seq", axis=0, tiled=True),
        lax.all_gather(ln2_gain, "seq", axis=0, tiled=True),
        lax.all_gather(ln2_bias, "seq", axis=0, tiled=True),
    )
    qkv_weight = gathered_weights[0]
    proj_weight = gathered_weights[1]
    router_weight = gathered_weights[2]
    gain_one = gathered_weights[3].astype(jnp.float32)
    bias_one = gathered_weights[4].astype(jnp.float32)
    gain_two = gathered_weights[5].astype(jnp.float32)
    bias_two = gathered_weights[6].astype(jnp.float32)
    inputs = tokens.astype(jnp.float32)
    row_count = inputs.shape[0]
    width = inputs.shape[1]
    normed_one, inverse_one = normalize(inputs)
    hidden_one = (normed_one * gain_one + bias_one).astype(jnp.bfloat16)
    qkv_local = jnp.dot(hidden_one, qkv_weight, preferred_element_type=jnp.float32).astype(
        jnp.bfloat16
    )
    heads_here = H // seq_count
    head_width = heads_here * HD
    length = row_count * seq_count
    qkv_heads = lax.all_to_all(
        qkv_local.reshape(row_count, 3, seq_count, head_width),
        "seq",
        split_axis=2,
        concat_axis=0,
        tiled=True,
    )
    queries = qkv_heads[:, 0, 0].reshape(length, heads_here, HD)
    key_rows = qkv_heads[:, 1, 0].reshape(length, heads_here, HD)
    value_rows = qkv_heads[:, 2, 0].reshape(length, heads_here, HD)
    starts = doc_starts[0]
    positions = jnp.arange(length, dtype=jnp.int32)
    doc_first = jnp.max(
        jnp.where(starts[None, :] <= positions[:, None], starts[None, :], 0), axis=1
    )
    block_rows = min(512, length)
    block_count = length // block_rows
    factor = HD ** (-0.5)

    def block_scores(block_index):
        begin = block_index * block_rows
        query_block = lax.dynamic_slice_in_dim(queries, begin, block_rows, 0)
        first_block = lax.dynamic_slice_in_dim(doc_first, begin, block_rows, 0)
        query_pos = begin + jnp.arange(block_rows, dtype=jnp.int32)
        allowed = (positions[None, :] <= query_pos[:, None]) & (
            positions[None, :] >= first_block[:, None]
        )
        scores = (
            jnp.einsum("qhd,khd->hqk", query_block, key_rows, preferred_element_type=jnp.float32)
            * factor
        )
        return jnp.where(allowed[None], scores, NEG)

    def forward_block(block_index):
        scores = block_scores(block_index)
        row_top = jnp.max(scores, axis=-1, keepdims=True)
        weights = jnp.exp(scores - row_top)
        totals = jnp.sum(weights, axis=-1, keepdims=True)
        probs_low = (weights / totals).astype(jnp.bfloat16)
        attended = jnp.einsum(
            "hqk,khd->qhd", probs_low, value_rows, preferred_element_type=jnp.float32
        ).astype(jnp.bfloat16)
        return (attended, (row_top + jnp.log(totals))[:, :, 0])

    attended_all, log_totals = lax.map(forward_block, jnp.arange(block_count, dtype=jnp.int32))
    heads_out = attended_all.reshape(length, head_width)
    token_heads = lax.all_to_all(heads_out, "seq", split_axis=0, concat_axis=1, tiled=True)
    middle = inputs + jnp.dot(token_heads, proj_weight, preferred_element_type=jnp.float32)
    normed_two, inverse_two = normalize(middle)
    hidden_two = (normed_two * gain_two + bias_two).astype(jnp.bfloat16)
    logits = jnp.dot(hidden_two, router_weight, preferred_element_type=jnp.float32)
    logit_top = jnp.max(logits, axis=-1, keepdims=True)
    logit_exp = jnp.exp(logits - logit_top)
    probs = logit_exp / jnp.sum(logit_exp, axis=-1, keepdims=True)
    expert_ids = routes[:, 0]
    expert_range = jnp.arange(EXPERTS, dtype=jnp.int32)
    selector = expert_ids[:, None] == expert_range[None, :]
    selector_float = selector.astype(jnp.float32)
    gate = jnp.sum(probs * selector_float, axis=1)
    capacity = max(2, 2 * TOK_DEV // EXPERTS)
    onehot_int = selector.astype(jnp.int32)
    ranking = jnp.sum((jnp.cumsum(onehot_int, axis=0) - 1) * onehot_int, axis=1)
    slot_ids = expert_ids * capacity + ranking
    placement_map = (
        jnp.arange(EXPERTS * capacity, dtype=jnp.int32)[:, None] == slot_ids[None, :]
    ).astype(jnp.bfloat16)
    grad_out = out_grad.astype(jnp.float32)
    scaled_grad = (gate[:, None] * grad_out).astype(jnp.bfloat16)
    local_experts = EXPERTS // dp_count
    buffer_shape = (dp_count, 1, local_experts, capacity, width)
    send_rows = (
        jnp.dot(placement_map, hidden_two, preferred_element_type=jnp.float32)
        .astype(jnp.bfloat16)
        .reshape(buffer_shape)
    )
    send_grads = (
        jnp.dot(placement_map, scaled_grad, preferred_element_type=jnp.float32)
        .astype(jnp.bfloat16)
        .reshape(buffer_shape)
    )
    collected = collect_rows(send_rows, send_grads)
    arrived = route_rows(collected[0], collected[1])
    part_out, part_dx, expert_in_grad, expert_out_grad = expert_work(
        arrived[0], arrived[1], w_expert_in, w_expert_out
    )
    summed_rows = (
        lax.psum_scatter(
            part_out.astype(jnp.bfloat16), "seq", scatter_dimension=1, tiled=True
        ).astype(jnp.float32),
        lax.psum_scatter(
            part_dx.astype(jnp.bfloat16), "seq", scatter_dimension=1, tiled=True
        ).astype(jnp.float32),
    )
    rows_out = summed_rows[0]
    rows_dx = summed_rows[1]
    back_rows = (
        lax.all_to_all(
            rows_out.astype(jnp.bfloat16), "dp", split_axis=0, concat_axis=0, tiled=True
        ),
        lax.all_to_all(rows_dx.astype(jnp.bfloat16), "dp", split_axis=0, concat_axis=0, tiled=True),
    )
    flat_out = back_rows[0].reshape(EXPERTS * capacity, width)
    flat_dx = back_rows[1].reshape(EXPERTS * capacity, width)
    expert_out = jnp.einsum(
        "sr,sd->rd", placement_map, flat_out, preferred_element_type=jnp.float32
    )
    expert_dx = jnp.einsum("sr,sd->rd", placement_map, flat_dx, preferred_element_type=jnp.float32)
    output = (middle + gate[:, None] * expert_out).astype(jnp.bfloat16)
    grad_gate = jnp.sum(grad_out * expert_out, axis=1)
    grad_logits = probs * (selector_float - gate[:, None]) * grad_gate[:, None]
    router_grad = jnp.dot(
        hidden_two.astype(jnp.float32).T, grad_logits, precision=lax.Precision.HIGHEST
    )
    grad_two = expert_dx + jnp.dot(
        grad_logits, router_weight.astype(jnp.float32).T, precision=lax.Precision.HIGHEST
    )
    gain_two_grad = jnp.sum(grad_two * normed_two, axis=0)
    bias_two_grad = jnp.sum(grad_two, axis=0)
    grad_middle = grad_out + norm_back(grad_two * gain_two, normed_two, inverse_two)
    grad_branch = grad_middle.astype(jnp.bfloat16)
    proj_grad = jnp.dot(token_heads.T, grad_branch, preferred_element_type=jnp.float32)
    grad_heads_tok = jnp.dot(grad_branch, proj_weight.T, preferred_element_type=jnp.float32).astype(
        jnp.bfloat16
    )
    grad_heads = lax.all_to_all(grad_heads_tok, "seq", split_axis=1, concat_axis=0, tiled=True)
    grad_attended = grad_heads.reshape(length, heads_here, HD)

    def backward_block(carry, block_index):
        key_acc, value_acc = carry
        begin = block_index * block_rows
        query_block = lax.dynamic_slice_in_dim(queries, begin, block_rows, 0)
        grad_block = lax.dynamic_slice_in_dim(grad_attended, begin, block_rows, 0)
        scores = block_scores(block_index)
        probs_block = jnp.exp(scores - log_totals[block_index][:, :, None])
        grad_probs = jnp.einsum(
            "qhd,khd->hqk", grad_block, value_rows, preferred_element_type=jnp.float32
        )
        row_dot = jnp.sum(probs_block * grad_probs, axis=-1, keepdims=True)
        grad_scores = (probs_block * (grad_probs - row_dot)).astype(jnp.bfloat16)
        grad_query = (
            jnp.einsum("hqk,khd->qhd", grad_scores, key_rows, preferred_element_type=jnp.float32)
            * factor
        ).astype(jnp.bfloat16)
        key_acc = (
            key_acc
            + jnp.einsum(
                "hqk,qhd->khd", grad_scores, query_block, preferred_element_type=jnp.float32
            )
            * factor
        )
        value_acc = value_acc + jnp.einsum(
            "hqk,qhd->khd",
            probs_block.astype(jnp.bfloat16),
            grad_block,
            preferred_element_type=jnp.float32,
        )
        return ((key_acc, value_acc), grad_query)

    zero_rows = jnp.zeros((length, heads_here, HD), jnp.float32)
    carried, query_grad = lax.scan(
        backward_block, (zero_rows, zero_rows), jnp.arange(block_count, dtype=jnp.int32)
    )
    grad_qkv_heads = jnp.stack(
        [
            query_grad.reshape(length, head_width),
            carried[0].astype(jnp.bfloat16).reshape(length, head_width),
            carried[1].astype(jnp.bfloat16).reshape(length, head_width),
        ],
        axis=1,
    )[:, :, None, :]
    grad_qkv = lax.all_to_all(
        grad_qkv_heads, "seq", split_axis=0, concat_axis=2, tiled=True
    ).reshape(row_count, 3 * width)
    qkv_grad = jnp.dot(hidden_one.T, grad_qkv, preferred_element_type=jnp.float32)
    grad_one = jnp.dot(grad_qkv, qkv_weight.T, preferred_element_type=jnp.float32)
    gain_one_grad = jnp.sum(grad_one * normed_one, axis=0)
    bias_one_grad = jnp.sum(grad_one, axis=0)
    input_grad = grad_middle + norm_back(grad_one * gain_one, normed_one, inverse_one)
    summed = (
        lax.psum_scatter(
            qkv_grad.astype(jnp.bfloat16), "seq", scatter_dimension=0, tiled=True
        ).astype(jnp.float32),
        lax.psum_scatter(
            proj_grad.astype(jnp.bfloat16), "seq", scatter_dimension=0, tiled=True
        ).astype(jnp.float32),
        lax.psum_scatter(
            router_grad.astype(jnp.bfloat16), "seq", scatter_dimension=0, tiled=True
        ).astype(jnp.float32),
        lax.psum_scatter(
            gain_one_grad.astype(jnp.bfloat16), "seq", scatter_dimension=0, tiled=True
        ).astype(jnp.float32),
        lax.psum_scatter(
            bias_one_grad.astype(jnp.bfloat16), "seq", scatter_dimension=0, tiled=True
        ).astype(jnp.float32),
        lax.psum_scatter(
            gain_two_grad.astype(jnp.bfloat16), "seq", scatter_dimension=0, tiled=True
        ).astype(jnp.float32),
        lax.psum_scatter(
            bias_two_grad.astype(jnp.bfloat16), "seq", scatter_dimension=0, tiled=True
        ).astype(jnp.float32),
    )
    reduced = (
        lax.psum(summed[0].astype(jnp.bfloat16), "dp").astype(jnp.float32),
        lax.psum(summed[1].astype(jnp.bfloat16), "dp").astype(jnp.float32),
        lax.psum(summed[2].astype(jnp.bfloat16), "dp").astype(jnp.float32),
        lax.psum(summed[3].astype(jnp.bfloat16), "dp").astype(jnp.float32),
        lax.psum(summed[4].astype(jnp.bfloat16), "dp").astype(jnp.float32),
        lax.psum(summed[5].astype(jnp.bfloat16), "dp").astype(jnp.float32),
        lax.psum(summed[6].astype(jnp.bfloat16), "dp").astype(jnp.float32),
    )
    return (
        output,
        input_grad,
        reduced[3],
        reduced[4],
        reduced[0],
        reduced[1],
        reduced[5],
        reduced[6],
        reduced[2],
        expert_in_grad,
        expert_out_grad,
    )


def solution(mesh):
    in_specs = (
        P(("dp", "seq"), None),
        P("dp", None),
        P(("dp", "seq"), None),
        P("seq"),
        P("seq"),
        P("seq", None),
        P("seq", None),
        P("seq"),
        P("seq"),
        P("seq", None),
        P("dp", None, "seq"),
        P("dp", "seq", None),
        P(("dp", "seq"), None),
    )
    out_specs = (
        P(("dp", "seq"), None),
        P(("dp", "seq"), None),
        P("seq"),
        P("seq"),
        P("seq", None),
        P("seq", None),
        P("seq"),
        P("seq"),
        P("seq", None),
        P("dp", None, "seq"),
        P("dp", "seq", None),
    )
    return jax.shard_map(
        per_device, mesh=mesh, in_specs=in_specs, out_specs=out_specs, check_vma=False
    )
```

profile of v0, /device:TPU:0, one launch (start us, length us, event | category | flops | bytes accessed | tf_op | source)
XLA Modules:
  0.0 1636.1 jit_solution(8930138773344012550)
XLA Ops:
  24.0 34.7 %all-gather.9.cloned.1.call-done = bf16[1024,3072]{1,0:T(8,128)(2,1)} async-done(((bf16[256,3072]{1,0:T(8,128)(2,1)}), bf16[1024,3072]{1,0:T(8,128)(2,1)}) %all-gather.9.cloned.1.call-update) | async-done | bytes 6291472 | tf_op jit(solution)/shard_map/all_gather | solution.py:83
  79.4 47.3 %all-to-all-done = bf16[512,3,4,256]{3,0,1,2:T(8,128)(2,1)S(1)} async-done(((bf16[512,3,4,256]{3,0,1,2:T(8,128)(2,1)}), bf16[512,3,4,256]{3,0,1,2:T(8,128)(2,1)S(1)}, u32[]{:S(2)}, u32[]{:S(2)}) %all-to-all-start) | async-done | bytes 3145760 | tf_op jit(solution)/shard_map/all_to_all | solution.py:109
  131.9 67.1 %while.30 = (s32[]{:T(128)}, bf16[4,512,4,64]{1,3,2,0:T(8,128)(2,1)}, f32[4,4,512]{2,1,0:T(4,128)}, s32[4]{0:T(128)S(1)}, s32[2048]{0:T(1024)S(1)}, /*index=5*/b...) while((s32[]{:T(128)}, ...), condition=%wide.region_6.7_spmd.clone.clone, body=%wide.region_3.6_spmd.clone.clone.sunk | while | flops 1127348736 | bytes 57223368 | solution.py:153
  203.3 15.3 all-gather.3
  232.5 58.4 %all-gather.13.cloned.1.call-done = bf16[8,4,8,16,1024]{4,3,1,2,0:T(8,128)(2,1)} async-done(((bf16[8,1,8,16,1024]{4,3,1,2,0:T(8,128)(2,1)}), bf16[8,4,8,16,1024]{4,3,1,2,0:T(8,128)(2,1)}) %all-gather.13.cloned.1.call-update) | async-done | bytes 8388624 | tf_op jit(solution)/shard_map/all_gather | solution.py:28
  307.7 58.9 %all-gather.15.cloned.1.call-done = bf16[8,4,8,16,1024]{4,3,1,2,0:T(8,128)(2,1)} async-done(((bf16[8,1,8,16,1024]{4,3,1,2,0:T(8,128)(2,1)}), bf16[8,4,8,16,1024]{4,3,1,2,0:T(8,128)(2,1)}) %all-gather.15.cloned.1.call-update) | async-done | bytes 8388624 | tf_op jit(solution)/shard_map/all_gather | solution.py:29
  366.6 113.5 %all-to-all-done.2 = bf16[8,4,8,16,1024]{4,3,1,2,0:T(8,128)(2,1)} async-done(((bf16[8,4,8,16,1024]{4,3,1,2,0:T(8,128)(2,1)}), bf16[8,4,8,16,1024]{4,3,1,2,0:T(8,128)(2,1)}, u32[]{:S(2)}, u32[]{:S(2)}) %all-to-all-start.2) | async-done | bytes 8388640 | tf_op jit(solution)/shard_map/all_to_all | solution.py:35
  485.3 24.4 %fusion.62 = (bf16[8,4,8,16,1024]{4,3,1,0,2:T(8,128)(2,1)}, f32[8,8,4,16,1024]{4,3,2,1,0:T(8,128)}) fusion(bf16[8,1024,1024]{2,1,0:T(8,128)(2,1)} %param.27, bf16[8,4,8,16,1024]{4,3,1,2,0:T(8,128)(2,1)} %all-to-all-done.2), kind=kOutput, calls=%fused_computation.76 | convolution fusion | flops 8627683328 | bytes 50331648 | tf_op jit(solution)/shard_map/abecd,edf->abecf/dot_general | solution.py:41
  509.7 158.0 %all-to-all-done.4 = bf16[8,4,8,16,1024]{4,3,1,2,0:T(8,128)(2,1)} async-done(((bf16[8,4,8,16,1024]{4,3,1,2,0:T(8,128)(2,1)}), bf16[8,4,8,16,1024]{4,3,1,2,0:T(8,128)(2,1)}, u32[]{:S(2)}, u32[]{:S(2)}) %all-to-all-start.4) | async-done | bytes 8388640 | tf_op jit(solution)/shard_map/all_to_all | solution.py:36
  667.6 25.7 %fusion.50 = bf16[8,4,8,16,1024]{4,3,1,0,2:T(8,128)(2,1)} fusion(f32[8,8,4,16,1024]{4,3,2,1,0:T(8,128)} %get-tuple-element.341, bf16[8,1024,1024]{2,1,0:T(8,128)(2,1)} %param.28, bf16[8,4,8,16,1024]{4,3,1,2,0:T(8,128)(2,1)} %all-to-all-done.4), kind=kOutput, calls=%fused_computation.61 | convolution fusion | flops 8673820672 | bytes 50331648 | tf_op jit(solution)/shard_map/abecd,efd->abecf/dot_general | solution.py:49
  693.4 15.9 convert_bitcast_fusion
  709.3 18.1 %convert_bitcast_fusion.1 = bf16[8,4,8,16,1024]{4,3,1,0,2:T(8,128)(2,1)} fusion(bf16[8,4,8,16,1024]{4,3,1,0,2:T(8,128)(2,1)} %get-tuple-element.340, bf16[8,1024,1024]{2,1,0:T(8,128)(2,1)} %param.28), kind=kOutput, calls=%fused_computation.84 | convolution fusion | flops 8594128896 | bytes 33554432 | tf_op jit(solution)/shard_map/abecf,efd->abecd/dot_general | solution.py:46
  728.6 285.9 %all-reduce.15.cloned.1.call-done = (bf16[8,4,8,16,1024]{4,3,1,0,2:T(8,128)(2,1)}, bf16[8,4,8,16,1024]{4,3,1,0,2:T(8,128)(2,1)}) async-done(((bf16[8,4,8,16,1024]{4,3,1,0,2:T(8,128)(2,1)}, bf16[8,4,8,16,1024]{4,3,1,0,2:T(8,128)(2,1)}), (bf16[8,4,8,16,1024]{4,3,1,0,2:T(8,128)(2,1)}, bf16[8,4,8,16,1024]{4,3,1,0,2:T(8,128)(2,1)})) %all-reduce.15.cloned.1.call-update) | async-done | bytes 16777232
  1027.9 44.4 %all-to-all-done.3 = bf16[8,1,8,16,1024]{4,3,1,2,0:T(8,128)(2,1)} async-done(((bf16[8,1,8,16,1024]{4,3,1,2,0:T(8,128)(2,1)}), bf16[8,1,8,16,1024]{4,3,1,2,0:T(8,128)(2,1)}, u32[]{:S(2)}, u32[]{:S(2)}) %all-to-all-start.3) | async-done | bytes 2097184 | tf_op jit(solution)/shard_map/all_to_all | solution.py:205
  1081.6 43.3 %all-to-all-done.5 = bf16[8,1,8,16,1024]{4,3,1,2,0:T(8,128)(2,1)} async-done(((bf16[8,1,8,16,1024]{4,3,1,2,0:T(8,128)(2,1)}), bf16[8,1,8,16,1024]{4,3,1,2,0:T(8,128)(2,1)}, u32[]{:S(2)}, u32[]{:S(2)}) %all-to-all-start.5) | async-done | bytes 2097184 | tf_op jit(solution)/shard_map/all_to_all | solution.py:208
  1156.3 203.1 %while.31 = (s32[]{:T(128)}, f32[2048,4,64]{0,2,1:T(8,128)}, f32[2048,4,64]{0,2,1:T(8,128)}, bf16[4,512,4,64]{1,3,2,0:T(8,128)(2,1)}, s32[4]{0:T(128)S(1)}, /*in...) while((s32[]{:T(128)}, f32[2048,4,64]{0,2,1:T(8,128)}, ...), condition=%wide.region_22.23_spmd.clone.clone, body=%wide.region_20.22_spmd.clone.clone.sunk | while | flops 2753296896 | bytes 184945072 | solution.py:268
  1172.8 11.6 multiply_reduce_fusion.7
  1325.0 11.5 multiply_reduce_fusion.7
  1370.3 51.9 %all_to_all.88 = bf16[2048,3,1,256]{3,1,2,0:T(4,128)(2,1)S(1)} all-to-all(bf16[2048,3,1,256]{3,1,2,0:T(4,128)(2,1)} %copy.112), channel_id=1, replica_groups=mesh['dp'=8,'seq'=4] {'seq'}, dimensions={0} | all-to-all | bytes 6291456 | tf_op jit(solution)/shard_map/all_to_all | solution.py:279
  1439.7 23.5 %convolution_bitcast_fusion = f32[8,1024,1024]{2,1,0:T(8,128)} fusion(bf16[8,4,8,16,1024]{4,3,1,2,0:T(8,128)(2,1)} %all-to-all-done.4, bf16[8,4,8,16,1024]{4,3,1,0,2:T(8,128)(2,1)} %get-tuple-element.340), kind=kOutput, calls=%fused_computation.77 | convolution fusion | flops 8589934592 | bytes 50331648 | tf_op jit(solution)/shard_map/abecf,abecd->efd/dot_general | solution.py:56
  1463.2 30.5 %reduce-scatter.10.cloned.1.call-done = bf16[256,3072]{1,0:T(8,128)(2,1)} async-done(((bf16[1024,3072]{1,0:T(8,128)(2,1)}), bf16[256,3072]{1,0:T(8,128)(2,1)}) %reduce-scatter.10.cloned.1.call-update) | async-done | bytes 1572880 | tf_op jit(solution)/shard_map/reduce_scatter | solution.py:288
  1493.7 20.0 %convolution_bitcast_fusion.1 = f32[8,1024,1024]{2,1,0:T(8,128)} fusion(bf16[8,4,8,16,1024]{4,3,1,2,0:T(8,128)(2,1)} %all-to-all-done.2, bf16[8,4,8,16,1024]{4,3,1,0,2:T(8,128)(2,1)} %fusion.50), kind=kOutput, calls=%fused_computation.78 | convolution fusion | flops 8589934592 | bytes 50331648 | tf_op jit(solution)/shard_map/abecd,abecf->edf/dot_general | solution.py:53
  1529.2 39.4 %all-reduce.6 = (bf16[256]{0:T(256)(128)(2,1)S(1)}, bf16[256]{0:T(256)(128)(2,1)S(1)}, bf16[256]{0:T(256)(128)(2,1)S(1)}, bf16[256]{0:T(256)(128)(2,1)S(1)}, bf16[256,64]{0,1:T(8,128)(2,1)S(1)}) all-reduce(bf16[256]{0:T(256)(128)(2,1)S(1)} %dynamic-slice.5, ...), channel_id=1, replica_groups=mesh['dp'=8,'seq'=4] {'dp'}, use_global_device_ids=true, to_apply=%region_27.28 | all-reduce | flops 17408 | bytes 69632 | tf_op jit(solution)/shard_map/psum | solution.py:314
  1575.1 48.5 %all-reduce.13.cloned.1.call-done = (bf16[256,3072]{1,0:T(8,128)(2,1)}, bf16[256,1024]{1,0:T(8,128)(2,1)}) async-done(((bf16[256,3072]{1,0:T(8,128)(2,1)}, bf16[256,1024]{1,0:T(8,128)(2,1)}), (bf16[256,3072]{1,0:T(8,128)(2,1)}, bf16[256,1024]{1,0:T(8,128)(2,1)})) %all-reduce.13.cloned.1.call-update) | async-done | bytes 2097168 | tf_op jit(solution)/shard_map/psum | solution.py:311
  (320 shorter events, 426.1 us)
Async XLA Ops:
  7.2 51.5 %all-gather.9.cloned.1.call-start = ((), (), s32[]{:S(2)}) async-start(), calls=%async_computation.11 | async-start | bytes 7864320 | tf_op jit(solution)/shard_map/all_gather | solution.py:83
  74.7 52.0 %all-to-all-start = ((bf16[512,3,4,256]{3,0,1,2:T(8,128)(2,1)}), bf16[512,3,4,256]{3,0,1,2:T(8,128)(2,1)S(1)}, u32[]{:S(2)}, u32[]{:S(2)}) async-start(bf16[512,3,4,256]{3,0,1,2:T(8,128)(2,1)} %copy.97), calls=%async_computation | async-start | bytes 6291456 | tf_op jit(solution)/shard_map/all_to_all | solution.py:109
  78.5 147.0 %all-gather.11.cloned.1.call-start = ((), (), s32[]{:S(2)}) async-start(), calls=%async_computation.12 | async-start | bytes 2621440 | tf_op jit(solution)/shard_map/all_gather | solution.py:84
  131.9 71.4 %copy-start.45 = (bf16[256]{0:T(256)(128)(2,1)S(1)}, bf16[256]{0:T(256)(128)(2,1)}, u32[]{:S(2)}) copy-start(bf16[256]{0:T(256)(128)(2,1)} %param.24) | copy-start | bytes 1540
  131.9 71.4 %copy-start.46 = (bf16[256]{0:T(256)(128)(2,1)S(1)}, bf16[256]{0:T(256)(128)(2,1)}, u32[]{:S(2)}) copy-start(bf16[256]{0:T(256)(128)(2,1)} %param.25) | copy-start | bytes 1540
  131.9 91.9 %copy-start.20 = (s32[512,1]{0,1:T(1,128)S(1)}, s32[512,1]{0,1:T(1,128)}, u32[]{:S(2)}) copy-start(s32[512,1]{0,1:T(1,128)} %param.19) | copy-start | bytes 6148
  199.0 26.5 %all-to-all-start.1 = ((bf16[4,512,256]{1,2,0:T(8,128)(2,1)}), bf16[4,512,256]{1,2,0:T(8,128)(2,1)}, u32[]{:S(2)}, u32[]{:S(2)}) async-start(bf16[4,512,256]{1,2,0:T(8,128)(2,1)} %bitcast.224), calls=%async_computation.1 | async-start | bytes 2097152 | tf_op jit(solution)/shard_map/all_to_all | solution.py:155
  203.2 87.7 %all-gather.13.cloned.1.call-start = ((), (), s32[]{:S(2)}) async-start(), calls=%async_computation.13 | async-start | bytes 10485760 | tf_op jit(solution)/shard_map/all_gather | solution.py:28
  232.5 64.0 %copy-start.24 = (bf16[256,64]{0,1:T(8,128)(2,1)S(1)}, bf16[256,64]{0,1:T(8,128)(2,1)}, u32[]{:S(2)}) copy-start(bf16[256,64]{0,1:T(8,128)(2,1)} %param.26) | copy-start | bytes 98308
  290.9 189.1 %all-to-all-start.2 = ((bf16[8,4,8,16,1024]{4,3,1,2,0:T(8,128)(2,1)}), bf16[8,4,8,16,1024]{4,3,1,2,0:T(8,128)(2,1)}, u32[]{:S(2)}, u32[]{:S(2)}) async-start(bf16[8,4,8,16,1024]{4,3,1,2,0:T(8,128)(2,1)} %all-gather.13.cloned.1.call-done), calls=%async_computation.2 | async-start | bytes 16777216 | tf_op jit(solution)/shard_map/all_to_all | solution.py:35
  296.4 70.1 %all-gather.15.cloned.1.call-start = ((), (), s32[]{:S(2)}) async-start(), calls=%async_computation.14 | async-start | bytes 10485760 | tf_op jit(solution)/shard_map/all_gather | solution.py:29
  303.6 824.2 %copy-start.13 = (f32[512,64]{0,1:T(8,128)}, f32[512,64]{0,1:T(8,128)S(1)}, u32[]{:S(2)}) copy-start(f32[512,64]{0,1:T(8,128)S(1)} %get-tuple-element.343) | copy-start | bytes 393220
  303.6 824.2 %copy-start.22 = (f32[512]{0:T(512)}, f32[512]{0:T(512)S(1)}, u32[]{:S(2)}) copy-start(f32[512]{0:T(512)S(1)} %get-tuple-element.342) | copy-start | bytes 6148
  303.7 824.2 %copy-start.25 = (f32[512]{0:T(512)}, f32[512]{0:T(512)S(1)}, u32[]{:S(2)}) copy-start(f32[512]{0:T(512)S(1)} %fusion.107) | copy-start | bytes 6148
  303.7 826.6 %copy-start.27 = (f32[512]{0:T(512)}, f32[512]{0:T(512)S(1)}, u32[]{:S(2)}) copy-start(f32[512]{0:T(512)S(1)} %select_reduce_fusion) | copy-start | bytes 6148
  480.0 187.6 %all-to-all-start.4 = ((bf16[8,4,8,16,1024]{4,3,1,2,0:T(8,128)(2,1)}), bf16[8,4,8,16,1024]{4,3,1,2,0:T(8,128)(2,1)}, u32[]{:S(2)}, u32[]{:S(2)}) async-start(bf16[8,4,8,16,1024]{4,3,1,2,0:T(8,128)(2,1)} %all-gather.15.cloned.1.call-done), calls=%async_computation.4 | async-start | bytes 16777216 | tf_op jit(solution)/shard_map/all_to_all | solution.py:36
  485.0 529.5 %all-reduce.15.cloned.1.call-start = ((), (), s32[]{:S(2)}) async-start(), calls=%async_computation.19 | async-start | bytes 33554432
  1018.4 53.8 %all-to-all-start.3 = ((bf16[8,1,8,16,1024]{4,3,1,2,0:T(8,128)(2,1)}), bf16[8,1,8,16,1024]{4,3,1,2,0:T(8,128)(2,1)}, u32[]{:S(2)}, u32[]{:S(2)}) async-start(bf16[8,1,8,16,1024]{4,3,1,2,0:T(8,128)(2,1)} %copy.105), calls=%async_computation.3 | async-start | bytes 4194304 | tf_op jit(solution)/shard_map/all_to_all | solution.py:205
  1072.3 52.6 %all-to-all-start.5 = ((bf16[8,1,8,16,1024]{4,3,1,2,0:T(8,128)(2,1)}), bf16[8,1,8,16,1024]{4,3,1,2,0:T(8,128)(2,1)}, u32[]{:S(2)}, u32[]{:S(2)}) async-start(bf16[8,1,8,16,1024]{4,3,1,2,0:T(8,128)(2,1)} %copy.108), calls=%async_computation.5 | async-start | bytes 4194304 | tf_op jit(solution)/shard_map/all_to_all | solution.py:208
  1134.6 18.0 %all-to-all-start.6 = ((bf16[512,4,256]{2,0,1:T(8,128)(2,1)}), bf16[512,4,256]{2,0,1:T(8,128)(2,1)S(1)}, u32[]{:S(2)}, u32[]{:S(2)}) async-start(bf16[512,4,256]{2,0,1:T(8,128)(2,1)} %bitcast.187), calls=%async_computation.6 | async-start | bytes 2097152 | tf_op jit(solution)/shard_map/all_to_all | solution.py:233
  1138.1 325.0 %reduce-scatter.12.cloned.1.call-start = ((), (), s32[]{:S(2)}) async-start(), calls=%async_computation.16 | async-start | bytes 2621440 | tf_op jit(solution)/shard_map/reduce_scatter | solution.py:291
  1142.7 350.9 %reduce-scatter.10.cloned.1.call-start = ((), (), s32[]{:S(2)}) async-start(), calls=%async_computation.15 | async-start | bytes 7864320 | tf_op jit(solution)/shard_map/reduce_scatter | solution.py:288
  1437.0 92.1 %reduce-scatter.14.cloned.1.call-start = ((), (), s32[]{:S(2)}) async-start(), calls=%async_computation.17 | async-start | bytes 163840 | tf_op jit(solution)/shard_map/reduce_scatter | solution.py:294
  1439.6 184.0 %all-reduce.13.cloned.1.call-start = ((), (), s32[]{:S(2)}) async-start(), calls=%async_computation.18 | async-start | bytes 4194304 | tf_op jit(solution)/shard_map/psum | solution.py:311
  (55 other events, 564.0 us)
Sparse Core Ops, SparseCore 0:
  9.6 49.0 all-gather.8
  80.9 35.3 all-gather.10
  232.6 58.2 all-gather.12
  307.8 58.7 all-gather.14
  727.5 286.9 all-reduce.14
  1142.8 30.8 reduce-scatter.11
  1437.2 56.4 reduce-scatter.9
  1496.7 19.5 reduce-scatter.13
  1520.4 103.1 all-reduce.12
where the time goes:
time: 1640 us
  waiting for transfers between devices  934 us (57%)
  matrix products  356 us (22%)
  blocking collectives  134 us (8%)
  other arithmetic  95.7 us (6%)
  local copies, waits for them, and re-layouts  53.1 us (3%)
  starting transfers between devices  33.5 us (2%)
    unnamed x10, waiting for transfers between devices  287 us
    all_to_all x1, waiting for transfers between devices, route_rows(): lax.all_to_all(grads_part, 'dp', split_axis=0, concat_axis=0, tiled=True)  158 us
    all_to_all x1, waiting for transfers between devices, route_rows(): lax.all_to_all(rows_part, 'dp', split_axis=0, concat_axis=0, tiled=True)  113 us
    all_gather x1, waiting for transfers between devices, collect_rows(): lax.all_gather(grads_part, 'seq', axis=1, tiled=True)  58.9 us
    all_gather x1, waiting for transfers between devices, collect_rows(): lax.all_gather(rows_part, 'seq', axis=1, tiled=True)  58.4 us
    all_to_all x1, blocking collectives, per_device(): lax.all_to_all(grad_qkv_heads, 'seq', split_axis=0, concat_axis=2, tiled=...  51.9 us
    psum x1, waiting for transfers between devices, per_device(): lax.psum(summed[0].astype(jnp.bfloat16), 'dp').astype(jnp.float32)  48.5 us
    all_to_all x1, waiting for transfers between devices, per_device(): lax.all_to_all(qkv_local.reshape(row_count, 3, seq_count, head_width), 's...  47.3 us
  transfers between devices with their start and end apart: 16, of which 12 were waited for; matrix products, arithmetic and copies ran while one was open for 25% of the time, Pallas kernels for 0%

commit v1 on v0

--- a/solution.py
+++ b/solution.py
@@ -308,7 +308,7 @@
         ).astype(jnp.float32),
     )
     reduced = (
-        lax.psum(summed[0].astype(jnp.bfloat16), "dp").astype(jnp.float32),
+        jnp.sum(lax.all_gather(summed[0].astype(jnp.bfloat16), "dp"), axis=0).astype(jnp.float32),
         lax.psum(summed[1].astype(jnp.bfloat16), "dp").astype(jnp.float32),
         lax.psum(summed[2].astype(jnp.bfloat16), "dp").astype(jnp.float32),
         lax.psum(summed[3].astype(jnp.bfloat16), "dp").astype(jnp.float32),

time: 1640 us -> 1790 us (1.091)
  waiting for transfers between devices: 934 us -> 1080 us
    all_gather x0 -> x1, waiting for transfers between devices: none -> 174 us  [per_device(): lax.all_gather(summed[0].astype(jnp.bfloat16), 'dp')]
    psum x1, waiting for transfers between devices: 48.5 us -> 0.01 us  [per_device(): lax.psum(summed[1].astype(jnp.bfloat16), 'dp').astype(jnp.float32)]
    reduce_scatter x1, waiting for transfers between devices: 30.5 us -> 52.6 us  [per_device(): lax.psum_scatter(qkv_grad.astype(jnp.bfloat16), 'seq', scatter_dimension=...]
    unnamed x10 -> x11, waiting for transfers between devices: 287 us -> 288 us
  transfers between devices with their start and end apart: 16 -> 17, of which waited for: 12 -> 12; matrix products, arithmetic and copies ran while one was open for 25% -> 22% of each run, Pallas kernels for 0% -> 0%
where the time goes in v1:
time: 1790 us
  waiting for transfers between devices  1080 us (60%)
  matrix products  354 us (20%)
  blocking collectives  133 us (7%)
  other arithmetic  102 us (6%)
  local copies, waits for them, and re-layouts  53.8 us (3%)
  starting transfers between devices  32.9 us (2%)
    unnamed x11, waiting for transfers between devices  288 us
    all_gather x1, waiting for transfers between devices, per_device(): lax.all_gather(summed[0].astype(jnp.bfloat16), 'dp')  174 us
    all_to_all x1, waiting for transfers between devices, route_rows(): lax.all_to_all(grads_part, 'dp', split_axis=0, concat_axis=0, tiled=True)  158 us
    all_to_all x1, waiting for transfers between devices, route_rows(): lax.all_to_all(rows_part, 'dp', split_axis=0, concat_axis=0, tiled=True)  113 us
    all_gather x1, waiting for transfers between devices, collect_rows(): lax.all_gather(grads_part, 'seq', axis=1, tiled=True)  58.9 us
    all_gather x1, waiting for transfers between devices, collect_rows(): lax.all_gather(rows_part, 'seq', axis=1, tiled=True)  58.4 us
    reduce_scatter x1, waiting for transfers between devices, per_device(): lax.psum_scatter(qkv_grad.astype(jnp.bfloat16), 'seq', scatter_dimension=...  52.6 us
    all_to_all x1, blocking collectives, per_device(): lax.all_to_all(grad_qkv_heads, 'seq', split_axis=0, concat_axis=2, tiled=...  51.9 us
  transfers between devices with their start and end apart: 17, of which 12 were waited for; matrix products, arithmetic and copies ran while one was open for 22% of the time, Pallas kernels for 0%

profile of v1, /device:TPU:0, one launch (start us, length us, event | category | flops | bytes accessed | tf_op | source)
XLA Modules:
  0.0 1787.3 jit_solution(3253484305196933965)
XLA Ops:
  24.0 34.7 %all-gather.11.cloned.1.call-done = bf16[1024,3072]{1,0:T(8,128)(2,1)} async-done(((bf16[256,3072]{1,0:T(8,128)(2,1)}), bf16[1024,3072]{1,0:T(8,128)(2,1)}) %all-gather.11.cloned.1.call-update) | async-done | bytes 6291472 | tf_op jit(solution)/shard_map/all_gather | solution.py:83
  79.4 47.3 %all-to-all-done = bf16[512,3,4,256]{3,0,1,2:T(8,128)(2,1)S(1)} async-done(((bf16[512,3,4,256]{3,0,1,2:T(8,128)(2,1)}), bf16[512,3,4,256]{3,0,1,2:T(8,128)(2,1)S(1)}, u32[]{:S(2)}, u32[]{:S(2)}) %all-to-all-start) | async-done | bytes 3145760 | tf_op jit(solution)/shard_map/all_to_all | solution.py:109
  131.9 67.1 %while.30 = (s32[]{:T(128)}, bf16[4,512,4,64]{1,3,2,0:T(8,128)(2,1)}, f32[4,4,512]{2,1,0:T(4,128)}, s32[4]{0:T(128)S(1)}, s32[2048]{0:T(1024)S(1)}, /*index=5*/b...) while((s32[]{:T(128)}, ...), condition=%wide.region_6.7_spmd.clone.clone, body=%wide.region_3.6_spmd.clone.clone.sunk | while | flops 1127348736 | bytes 57223368 | solution.py:153
  203.3 15.3 all-gather.4
  232.5 58.4 %all-gather.15.cloned.1.call-done = bf16[8,4,8,16,1024]{4,3,1,2,0:T(8,128)(2,1)} async-done(((bf16[8,1,8,16,1024]{4,3,1,2,0:T(8,128)(2,1)}), bf16[8,4,8,16,1024]{4,3,1,2,0:T(8,128)(2,1)}) %all-gather.15.cloned.1.call-update) | async-done | bytes 8388624 | tf_op jit(solution)/shard_map/all_gather | solution.py:28
  307.7 58.9 %all-gather.17.cloned.1.call-done = bf16[8,4,8,16,1024]{4,3,1,2,0:T(8,128)(2,1)} async-done(((bf16[8,1,8,16,1024]{4,3,1,2,0:T(8,128)(2,1)}), bf16[8,4,8,16,1024]{4,3,1,2,0:T(8,128)(2,1)}) %all-gather.17.cloned.1.call-update) | async-done | bytes 8388624 | tf_op jit(solution)/shard_map/all_gather | solution.py:29
  366.6 113.5 %all-to-all-done.2 = bf16[8,4,8,16,1024]{4,3,1,2,0:T(8,128)(2,1)} async-done(((bf16[8,4,8,16,1024]{4,3,1,2,0:T(8,128)(2,1)}), bf16[8,4,8,16,1024]{4,3,1,2,0:T(8,128)(2,1)}, u32[]{:S(2)}, u32[]{:S(2)}) %all-to-all-start.2) | async-done | bytes 8388640 | tf_op jit(solution)/shard_map/all_to_all | solution.py:35
  485.3 24.4 %fusion.62 = (bf16[8,4,8,16,1024]{4,3,1,0,2:T(8,128)(2,1)}, f32[8,8,4,16,1024]{4,3,2,1,0:T(8,128)}) fusion(bf16[8,1024,1024]{2,1,0:T(8,128)(2,1)} %param.27, bf16[8,4,8,16,1024]{4,3,1,2,0:T(8,128)(2,1)} %all-to-all-done.2), kind=kOutput, calls=%fused_computation.76 | convolution fusion | flops 8627683328 | bytes 50331648 | tf_op jit(solution)/shard_map/abecd,edf->abecf/dot_general | solution.py:41
  509.8 157.9 %all-to-all-done.4 = bf16[8,4,8,16,1024]{4,3,1,2,0:T(8,128)(2,1)} async-done(((bf16[8,4,8,16,1024]{4,3,1,2,0:T(8,128)(2,1)}), bf16[8,4,8,16,1024]{4,3,1,2,0:T(8,128)(2,1)}, u32[]{:S(2)}, u32[]{:S(2)}) %all-to-all-start.4) | async-done | bytes 8388640 | tf_op jit(solution)/shard_map/all_to_all | solution.py:36
  667.7 25.9 %fusion.50 = bf16[8,4,8,16,1024]{4,3,1,0,2:T(8,128)(2,1)} fusion(f32[8,8,4,16,1024]{4,3,2,1,0:T(8,128)} %get-tuple-element.339, bf16[8,1024,1024]{2,1,0:T(8,128)(2,1)} %param.28, bf16[8,4,8,16,1024]{4,3,1,2,0:T(8,128)(2,1)} %all-to-all-done.4), kind=kOutput, calls=%fused_computation.61 | convolution fusion | flops 8673820672 | bytes 50331648 | tf_op jit(solution)/shard_map/abecd,efd->abecf/dot_general | solution.py:49
  693.6 16.3 convert_bitcast_fusion
  709.9 18.1 %convert_bitcast_fusion.1 = bf16[8,4,8,16,1024]{4,3,1,0,2:T(8,128)(2,1)} fusion(bf16[8,4,8,16,1024]{4,3,1,0,2:T(8,128)(2,1)} %get-tuple-element.338, bf16[8,1024,1024]{2,1,0:T(8,128)(2,1)} %param.28), kind=kOutput, calls=%fused_computation.84 | convolution fusion | flops 8594128896 | bytes 33554432 | tf_op jit(solution)/shard_map/abecf,efd->abecd/dot_general | solution.py:46
  729.2 285.9 %all-reduce.14.cloned.1.call-done = (bf16[8,4,8,16,1024]{4,3,1,0,2:T(8,128)(2,1)}, bf16[8,4,8,16,1024]{4,3,1,0,2:T(8,128)(2,1)}) async-done(((bf16[8,4,8,16,1024]{4,3,1,0,2:T(8,128)(2,1)}, bf16[8,4,8,16,1024]{4,3,1,0,2:T(8,128)(2,1)}), (bf16[8,4,8,16,1024]{4,3,1,0,2:T(8,128)(2,1)}, bf16[8,4,8,16,1024]{4,3,1,0,2:T(8,128)(2,1)})) %all-reduce.14.cloned.1.call-update) | async-done | bytes 16777232
  1028.5 44.4 %all-to-all-done.3 = bf16[8,1,8,16,1024]{4,3,1,2,0:T(8,128)(2,1)} async-done(((bf16[8,1,8,16,1024]{4,3,1,2,0:T(8,128)(2,1)}), bf16[8,1,8,16,1024]{4,3,1,2,0:T(8,128)(2,1)}, u32[]{:S(2)}, u32[]{:S(2)}) %all-to-all-start.3) | async-done | bytes 2097184 | tf_op jit(solution)/shard_map/all_to_all | solution.py:205
  1081.9 43.3 %all-to-all-done.5 = bf16[8,1,8,16,1024]{4,3,1,2,0:T(8,128)(2,1)} async-done(((bf16[8,1,8,16,1024]{4,3,1,2,0:T(8,128)(2,1)}), bf16[8,1,8,16,1024]{4,3,1,2,0:T(8,128)(2,1)}, u32[]{:S(2)}, u32[]{:S(2)}) %all-to-all-start.5) | async-done | bytes 2097184 | tf_op jit(solution)/shard_map/all_to_all | solution.py:208
  1156.7 203.5 %while.31 = (s32[]{:T(128)}, f32[2048,4,64]{0,2,1:T(8,128)}, f32[2048,4,64]{0,2,1:T(8,128)}, bf16[4,512,4,64]{1,3,2,0:T(8,128)(2,1)}, s32[4]{0:T(128)S(1)}, /*in...) while((s32[]{:T(128)}, f32[2048,4,64]{0,2,1:T(8,128)}, ...), condition=%wide.region_22.23_spmd.clone.clone, body=%wide.region_20.22_spmd.clone.clone.sunk | while | flops 2753296896 | bytes 184945072 | solution.py:268
  1173.2 11.5 multiply_reduce_fusion.7
  1274.5 11.5 multiply_reduce_fusion.7
  1371.1 51.9 %all_to_all.88 = bf16[2048,3,1,256]{3,1,2,0:T(4,128)(2,1)S(1)} all-to-all(bf16[2048,3,1,256]{3,1,2,0:T(4,128)(2,1)} %copy.112), channel_id=1, replica_groups=mesh['dp'=8,'seq'=4] {'seq'}, dimensions={0} | all-to-all | bytes 6291456 | tf_op jit(solution)/shard_map/all_to_all | solution.py:279
  1441.8 52.6 %reduce-scatter.10.cloned.1.call-done = bf16[256,3072]{1,0:T(8,128)(2,1)} async-done(((bf16[1024,3072]{1,0:T(8,128)(2,1)}), bf16[256,3072]{1,0:T(8,128)(2,1)}) %reduce-scatter.10.cloned.1.call-update) | async-done | bytes 1572880 | tf_op jit(solution)/shard_map/reduce_scatter | solution.py:288
  1494.4 20.9 %convolution_bitcast_fusion = f32[8,1024,1024]{2,1,0:T(8,128)} fusion(bf16[8,4,8,16,1024]{4,3,1,2,0:T(8,128)(2,1)} %all-to-all-done.4, bf16[8,4,8,16,1024]{4,3,1,0,2:T(8,128)(2,1)} %get-tuple-element.338), kind=kOutput, calls=%fused_computation.77 | convolution fusion | flops 8589934592 | bytes 50331648 | tf_op jit(solution)/shard_map/abecf,abecd->efd/dot_general | solution.py:56
  1515.3 19.9 %convolution_bitcast_fusion.1 = f32[8,1024,1024]{2,1,0:T(8,128)} fusion(bf16[8,4,8,16,1024]{4,3,1,2,0:T(8,128)(2,1)} %all-to-all-done.2, bf16[8,4,8,16,1024]{4,3,1,0,2:T(8,128)(2,1)} %fusion.50), kind=kOutput, calls=%fused_computation.78 | convolution fusion | flops 8589934592 | bytes 50331648 | tf_op jit(solution)/shard_map/abecd,abecf->edf/dot_general | solution.py:53
  1550.7 37.9 %all-reduce.6 = (bf16[256]{0:T(256)(128)(2,1)S(1)}, bf16[256]{0:T(256)(128)(2,1)S(1)}, bf16[256]{0:T(256)(128)(2,1)S(1)}, bf16[256]{0:T(256)(128)(2,1)S(1)}, bf16[256,64]{0,1:T(8,128)(2,1)S(1)}) all-reduce(bf16[256]{0:T(256)(128)(2,1)S(1)} %dynamic-slice.5, ...), channel_id=1, replica_groups=mesh['dp'=8,'seq'=4] {'dp'}, use_global_device_ids=true, to_apply=%region_27.28 | all-reduce | flops 17408 | bytes 69632 | tf_op jit(solution)/shard_map/psum | solution.py:314
  1597.2 173.8 %all-gather.19.cloned.1.call-done = bf16[2048,3072]{1,0:T(8,128)(2,1)} async-done(((bf16[256,3072]{1,0:T(8,128)(2,1)}), bf16[2048,3072]{1,0:T(8,128)(2,1)}) %all-gather.19.cloned.1.call-update) | async-done | bytes 12582928 | tf_op jit(solution)/shard_map/all_gather | solution.py:311
  (324 shorter events, 433.3 us)
Async XLA Ops:
  7.2 51.5 %all-gather.11.cloned.1.call-start = ((), (), s32[]{:S(2)}) async-start(), calls=%async_computation.11 | async-start | bytes 7864320 | tf_op jit(solution)/shard_map/all_gather | solution.py:83
  74.7 52.0 %all-to-all-start = ((bf16[512,3,4,256]{3,0,1,2:T(8,128)(2,1)}), bf16[512,3,4,256]{3,0,1,2:T(8,128)(2,1)S(1)}, u32[]{:S(2)}, u32[]{:S(2)}) async-start(bf16[512,3,4,256]{3,0,1,2:T(8,128)(2,1)} %copy.97), calls=%async_computation | async-start | bytes 6291456 | tf_op jit(solution)/shard_map/all_to_all | solution.py:109
  78.5 147.0 %all-gather.13.cloned.1.call-start = ((), (), s32[]{:S(2)}) async-start(), calls=%async_computation.12 | async-start | bytes 2621440 | tf_op jit(solution)/shard_map/all_gather | solution.py:84
  131.9 71.4 %copy-start.45 = (bf16[256]{0:T(256)(128)(2,1)S(1)}, bf16[256]{0:T(256)(128)(2,1)}, u32[]{:S(2)}) copy-start(bf16[256]{0:T(256)(128)(2,1)} %param.24) | copy-start | bytes 1540
  131.9 71.4 %copy-start.46 = (bf16[256]{0:T(256)(128)(2,1)S(1)}, bf16[256]{0:T(256)(128)(2,1)}, u32[]{:S(2)}) copy-start(bf16[256]{0:T(256)(128)(2,1)} %param.25) | copy-start | bytes 1540
  131.9 92.0 %copy-start.20 = (s32[512,1]{0,1:T(1,128)S(1)}, s32[512,1]{0,1:T(1,128)}, u32[]{:S(2)}) copy-start(s32[512,1]{0,1:T(1,128)} %param.19) | copy-start | bytes 6148
  199.0 26.6 %all-to-all-start.1 = ((bf16[4,512,256]{1,2,0:T(8,128)(2,1)}), bf16[4,512,256]{1,2,0:T(8,128)(2,1)}, u32[]{:S(2)}, u32[]{:S(2)}) async-start(bf16[4,512,256]{1,2,0:T(8,128)(2,1)} %bitcast.226), calls=%async_computation.1 | async-start | bytes 2097152 | tf_op jit(solution)/shard_map/all_to_all | solution.py:155
  203.2 87.7 %all-gather.15.cloned.1.call-start = ((), (), s32[]{:S(2)}) async-start(), calls=%async_computation.13 | async-start | bytes 10485760 | tf_op jit(solution)/shard_map/all_gather | solution.py:28
  291.0 189.1 %all-to-all-start.2 = ((bf16[8,4,8,16,1024]{4,3,1,2,0:T(8,128)(2,1)}), bf16[8,4,8,16,1024]{4,3,1,2,0:T(8,128)(2,1)}, u32[]{:S(2)}, u32[]{:S(2)}) async-start(bf16[8,4,8,16,1024]{4,3,1,2,0:T(8,128)(2,1)} %all-gather.15.cloned.1.call-done), calls=%async_computation.2 | async-start | bytes 16777216 | tf_op jit(solution)/shard_map/all_to_all | solution.py:35
  296.5 70.1 %all-gather.17.cloned.1.call-start = ((), (), s32[]{:S(2)}) async-start(), calls=%async_computation.14 | async-start | bytes 10485760 | tf_op jit(solution)/shard_map/all_gather | solution.py:29
  303.7 824.5 %copy-start.13 = (f32[512,64]{0,1:T(8,128)}, f32[512,64]{0,1:T(8,128)S(1)}, u32[]{:S(2)}) copy-start(f32[512,64]{0,1:T(8,128)S(1)} %get-tuple-element.341) | copy-start | bytes 393220
  303.7 824.5 %copy-start.22 = (f32[512]{0:T(512)}, f32[512]{0:T(512)S(1)}, u32[]{:S(2)}) copy-start(f32[512]{0:T(512)S(1)} %get-tuple-element.340) | copy-start | bytes 6148
  303.7 824.4 %copy-start.25 = (f32[512]{0:T(512)}, f32[512]{0:T(512)S(1)}, u32[]{:S(2)}) copy-start(f32[512]{0:T(512)S(1)} %fusion.107) | copy-start | bytes 6148
  303.8 826.9 %copy-start.27 = (f32[512]{0:T(512)}, f32[512]{0:T(512)S(1)}, u32[]{:S(2)}) copy-start(f32[512]{0:T(512)S(1)} %select_reduce_fusion) | copy-start | bytes 6148
  480.1 187.6 %all-to-all-start.4 = ((bf16[8,4,8,16,1024]{4,3,1,2,0:T(8,128)(2,1)}), bf16[8,4,8,16,1024]{4,3,1,2,0:T(8,128)(2,1)}, u32[]{:S(2)}, u32[]{:S(2)}) async-start(bf16[8,4,8,16,1024]{4,3,1,2,0:T(8,128)(2,1)} %all-gather.17.cloned.1.call-done), calls=%async_computation.4 | async-start | bytes 16777216 | tf_op jit(solution)/shard_map/all_to_all | solution.py:36
  485.0 530.1 %all-reduce.14.cloned.1.call-start = ((), (), s32[]{:S(2)}) async-start(), calls=%async_computation.20 | async-start | bytes 33554432
  1019.0 53.8 %all-to-all-start.3 = ((bf16[8,1,8,16,1024]{4,3,1,2,0:T(8,128)(2,1)}), bf16[8,1,8,16,1024]{4,3,1,2,0:T(8,128)(2,1)}, u32[]{:S(2)}, u32[]{:S(2)}) async-start(bf16[8,1,8,16,1024]{4,3,1,2,0:T(8,128)(2,1)} %copy.105), calls=%async_computation.3 | async-start | bytes 4194304 | tf_op jit(solution)/shard_map/all_to_all | solution.py:205
  1072.9 52.3 %all-to-all-start.5 = ((bf16[8,1,8,16,1024]{4,3,1,2,0:T(8,128)(2,1)}), bf16[8,1,8,16,1024]{4,3,1,2,0:T(8,128)(2,1)}, u32[]{:S(2)}, u32[]{:S(2)}) async-start(bf16[8,1,8,16,1024]{4,3,1,2,0:T(8,128)(2,1)} %copy.108), calls=%async_computation.5 | async-start | bytes 4194304 | tf_op jit(solution)/shard_map/all_to_all | solution.py:208
  1135.0 18.0 %all-to-all-start.6 = ((bf16[512,4,256]{2,0,1:T(8,128)(2,1)}), bf16[512,4,256]{2,0,1:T(8,128)(2,1)S(1)}, u32[]{:S(2)}, u32[]{:S(2)}) async-start(bf16[512,4,256]{2,0,1:T(8,128)(2,1)} %bitcast.188), calls=%async_computation.6 | async-start | bytes 2097152 | tf_op jit(solution)/shard_map/all_to_all | solution.py:233
  1138.5 301.9 %reduce-scatter.12.cloned.1.call-start = ((), (), s32[]{:S(2)}) async-start(), calls=%async_computation.16 | async-start | bytes 2621440 | tf_op jit(solution)/shard_map/reduce_scatter | solution.py:291
  1143.1 351.3 %reduce-scatter.10.cloned.1.call-start = ((), (), s32[]{:S(2)}) async-start(), calls=%async_computation.15 | async-start | bytes 7864320 | tf_op jit(solution)/shard_map/reduce_scatter | solution.py:288
  1437.8 112.9 %reduce-scatter.14.cloned.1.call-start = ((), (), s32[]{:S(2)}) async-start(), calls=%async_computation.18 | async-start | bytes 163840 | tf_op jit(solution)/shard_map/reduce_scatter | solution.py:294
  1440.3 154.7 %all-reduce.12.cloned.1.call-start = ((), (), s32[]{:S(2)}) async-start(), calls=%async_computation.17 | async-start | bytes 1048576 | tf_op jit(solution)/shard_map/psum | solution.py:312
  1441.1 329.9 %all-gather.19.cloned.1.call-start = ((), (), s32[]{:S(2)}) async-start(), calls=%async_computation.19 | async-start | bytes 14155776 | tf_op jit(solution)/shard_map/all_gather | solution.py:311
  (56 other events, 626.8 us)
Sparse Core Ops, SparseCore 0:
  9.6 49.0 all-gather.10
  80.9 35.3 all-gather.12
  232.6 58.2 all-gather.14
  307.8 58.7 all-gather.16
  728.1 286.9 all-reduce.13
  1143.2 30.8 reduce-scatter.11
  1437.9 56.4 reduce-scatter.9
  1497.4 19.5 reduce-scatter.13
  1520.8 72.3 all-reduce.11
  1595.2 175.7 all-gather.18
